TPU v7x, 32 devices: a whole 2x2x4 slice. The times are simulated.
32 devices in a mesh: rows: 8 (over y, x, core), cols: 4 (over z).
Axes of the slice: x: 2, y: 2, z: 4, core: 2. Of those that a mesh axis runs over, the one named last changes fastest.
Arguments:
- irradiance_layers: bfloat16 [2, 2048, 16384], P(None, ('rows', 'cols')), may hold values from 0 to 2
- initial_heat_anomaly: float32 [2, 2048, 16384], P(None, 'rows', 'cols'), may hold values from -12 to 12
- drift_rate_eastward: float32 [2, 2048, 16384], P(None, 'rows', 'cols'), may hold values from 0.35 to 0.45
- drift_rate_northward: float32 [2, 2048, 16384], P(None, 'rows', 'cols'), may hold values from 0.33 to 0.4
- extinction_factor: float32 [2, 2048, 16384], P(None, 'rows', 'cols'), may hold values from 0.1 to 1
- windward_polarity_eastward: int32 [2, 2048], P(None, 'rows'), may hold values from 0 to 1
- windward_polarity_northward: int32 [2, 16384], P(None, 'cols'), may hold values from 0 to 1
Outputs:
- phase_slabs: float32 [2, 2048, 16384], P(None, ('rows', 'cols'))
- temperature_end: float32 [2, 2048, 16384], P(None, 'rows', 'cols')
Inputs may be any that keep to these rules, and one draw needn't show every extreme that they name: `windward_polarity_eastward`: 1 means wind plus slew toward increasing x. `windward_polarity_northward`: 1 means wind plus slew toward increasing y.
All inputs are finite; a program needn't handle non-finite values.
Results may differ from a plain program's by a relative error of at most 0.0003.
Values may be sent and summed in bfloat16 or wider, within the bound.
No kernel may reach another device: no remote copies, remote signals or barrier semaphores. Data moves between devices by JAX's collectives and lax.ppermute only.
A program may use at most 192 MiB of HBM per device.

v0:
```python
import jax
import jax.numpy as jnp
from jax import lax
from jax.sharding import PartitionSpec as P

SUBSTEPS = 4
DIFFUSION = 0.03
HEAT_RATE = 0.25


def extended(block, sides, width):
    for axis, dim in sides:
        count = lax.axis_size(axis)
        forward = [(i, i + 1) for i in range(count - 1)]
        backward = [(target, source) for source, target in forward]
        low = lax.ppermute(
            lax.slice_in_dim(block, block.shape[dim] - width, None, axis=dim), axis, forward
        )
        high = lax.ppermute(lax.slice_in_dim(block, 0, width, axis=dim), axis, backward)
        block = jnp.concatenate([low, block, high], axis=dim)
    return block


def advance(padded, wind_x, wind_y, heating):
    middle = padded[1:-1, 1:-1]
    west_cell = padded[1:-1, :-2]
    east_cell = padded[1:-1, 2:]
    south_cell = padded[:-2, 1:-1]
    north_cell = padded[2:, 1:-1]
    upwind_x = jnp.where(wind_x > 0, west_cell, east_cell)
    upwind_y = jnp.where(wind_y > 0, south_cell, north_cell)
    neighbours = west_cell + east_cell + south_cell + north_cell - 4.0 * middle
    return (
        middle
        - jnp.abs(wind_x) * (middle - upwind_x)
        - jnp.abs(wind_y) * (middle - upwind_y)
        + DIFFUSION * neighbours
        + heating
    )


def body(
    irradiance_layers,
    initial_heat_anomaly,
    drift_rate_eastward,
    drift_rate_northward,
    extinction_factor,
    windward_polarity_eastward,
    windward_polarity_northward,
):
    optical_layers = initial_heat_anomaly.shape[0]
    arrived = lax.all_to_all(irradiance_layers, "cols", split_axis=2, concat_axis=1, tiled=True)
    phases = []
    finals = []
    for optical_layer in range(optical_layers):
        light_tile = arrived[optical_layer]
        wind_x = jnp.where(
            windward_polarity_eastward[optical_layer][:, None] == 1,
            drift_rate_eastward[optical_layer],
            -drift_rate_eastward[optical_layer],
        )
        wind_y = jnp.where(
            windward_polarity_northward[optical_layer][None, :] == 1,
            drift_rate_northward[optical_layer],
            -drift_rate_northward[optical_layer],
        )
        heating = HEAT_RATE * extinction_factor[optical_layer] * light_tile.astype(jnp.float32)
        heat_transport_advance = initial_heat_anomaly[optical_layer]
        phase_sum = jnp.zeros_like(heat_transport_advance)
        for section_index in range(SUBSTEPS):
            padded = extended(heat_transport_advance, (("rows", 0), ("cols", 1)), 1)
            heat_transport_advance = advance(padded, wind_x, wind_y, heating)
            phase_sum = phase_sum + heat_transport_advance / SUBSTEPS
        phases.append(phase_sum)
        finals.append(heat_transport_advance)
    phase_slabs = lax.all_to_all(jnp.stack(phases), "cols", split_axis=1, concat_axis=2, tiled=True)
    return (phase_slabs, jnp.stack(finals))


def solution(mesh):
    return jax.shard_map(
        body,
        mesh=mesh,
        in_specs=(
            P(None, ("rows", "cols"), None),
            P(None, "rows", "cols"),
            P(None, "rows", "cols"),
            P(None, "rows", "cols"),
            P(None, "rows", "cols"),
            P(None, "rows"),
            P(None, "cols"),
        ),
        out_specs=(P(None, ("rows", "cols"), None), P(None, "rows", "cols")),
        check_vma=False,
    )
```

profile of v0, /device:TPU:3, one launch (start us, length us, event | category | flops | bytes accessed | tf_op | source)
XLA Modules:
  0.0 627.5 jit_solution(5142534280835631980)
XLA Ops:
  0.6 17.8 %copy.19 = bf16[2,64,16384]{1,0,2:T(2,128)(2,1)} copy(bf16[2,64,16384]{2,1,0:T(8,128)(2,1)} %param.7) | data formatting | bytes 8388608 | tf_op args[0]
  18.4 9.6 %reshape.44 = bf16[4,2,262144]{2,1,0:T(2,128)(2,1)} reshape(bf16[16384,2,64]{2,1,0:T(2,128)(2,1)} %bitcast.140) | data formatting | bytes 8388608
  28.0 5.0 all-to-all-start
  61.0 64.7 %all-to-all-done = bf16[4,2,262144]{2,1,0:T(2,128)(2,1)} async-done(((bf16[4,2,262144]{2,1,0:T(2,128)(2,1)}), bf16[4,2,262144]{2,1,0:T(2,128)(2,1)}, u32[]{:S(2)}, u32[]{:S(2)}) %all-to-all-start) | async-done | bytes 4194336 | tf_op jit(solution)/shard_map/all_to_all | solution.py:52
  125.6 9.3 %reshape.45 = bf16[16384,2,64]{2,1,0:T(2,128)(2,1)} reshape(bf16[4,2,262144]{2,1,0:T(2,128)(2,1)} %all-to-all-done) | data formatting | bytes 8388608
  134.9 18.6 %copy.21 = bf16[2,64,4,4096]{3,1,2,0:T(8,128)(2,1)} copy(bf16[2,64,4,4096]{1,0,3,2:T(2,128)(2,1)} %bitcast.139) | data formatting | bytes 8388608 | tf_op jit(solution)/shard_map/all_to_all | solution.py:52
  158.4 20.0 %add_add_fusion.7 = (f32[256,4096]{1,0:T(8,128)S(1)}, pred[256,4096]{1,0:T(8,128)(4,1)}, pred[256,4096]{1,0:T(8,128)(4,1)}) fusion(f32[256,4096]{1,0:T(8,128)} %copy-done.8, f32[1,4096]{1,0:T(1,128)S(1)} %collective-permute-done, f32[1,4096]{1,0:T(1,128)S(1)} %collective-permute-done.1, f32[258,1]{1,0:T(8,128)} %copy-done.12, f32[258,1]{1,0:T(8,128)} %copy-done.13, ...), kind=kLoop, calls=%fused_computation.82 | loop fusion | flops 36700160 | bytes 25205008 | tf_op jit(solution)/shard_map/add | solution.py:34
  178.5 5.6 collective-permute-start.4
  186.2 19.6 %add_add_fusion.3 = (f32[256,4096]{1,0:T(8,128)S(1)}, pred[256,4096]{1,0:T(8,128)(4,1)}, pred[256,4096]{1,0:T(8,128)(4,1)}) fusion(f32[256,4096]{1,0:T(8,128)} %copy-done.7, f32[1,4096]{1,0:T(1,128)S(1)} %collective-permute-done.16, f32[1,4096]{1,0:T(1,128)S(1)} %collective-permute-done.17, f32[258,1]{1,0:T(8,128)S(1)} %collective-permute-done.18, ...), kind=kLoop, calls=%fused_computation.76 | loop fusion | flops 36700160 | bytes 25205008 | tf_op jit(solution)/shard_map/add | solution.py:34
  221.9 12.6 %add_add_fusion.6 = f32[256,4096]{1,0:T(8,128)} fusion(f32[256,4096]{1,0:T(8,128)S(1)} %get-tuple-element.8, pred[256,4096]{1,0:T(8,128)(4,1)} %get-tuple-element.10, f32[1,4096]{1,0:T(1,128)S(1)} %collective-permute-done.4, f32[1,4096]{1,0:T(1,128)S(1)} %collective-permute-done.5, pred[256,4096]{1,0:T(8,128)(4,1)} %get-tuple-element.9, ...), kind=kLoop, calls=%fused_computation.81 | loop fusion | flops 34603008 | bytes 25205008 | tf_op jit(solution)/shard_map/add | solution.py:34
  236.2 5.1 collective-permute-start.8
  243.2 18.1 %add_add_fusion.2 = f32[256,4096]{1,0:T(8,128)} fusion(f32[256,4096]{1,0:T(8,128)} %copy-done, pred[256,4096]{1,0:T(8,128)(4,1)} %get-tuple-element.15, f32[1,4096]{1,0:T(1,128)S(1)} %collective-permute-done.20, f32[1,4096]{1,0:T(1,128)} %copy-done.22, pred[256,4096]{1,0:T(8,128)(4,1)} %get-tuple-element.14, f32[258,1]{1,0:T(8,128)S(1)} %collective-permute-done.22, ...), kind=kLoop, calls=%fused_computation.75 | loop fusion | flops 34603008 | bytes 25205008 | tf_op jit(solution)/shard_map/add | solution.py:34
  282.5 18.8 %add_add_fusion.5 = f32[256,4096]{1,0:T(8,128)} fusion(f32[256,4096]{1,0:T(8,128)} %add_add_fusion.6, pred[256,4096]{1,0:T(8,128)(4,1)} %get-tuple-element.10, f32[1,4096]{1,0:T(1,128)S(1)} %collective-permute-done.8, f32[1,4096]{1,0:T(1,128)S(1)} %collective-permute-done.9, pred[256,4096]{1,0:T(8,128)(4,1)} %get-tuple-element.9, f32[258,1]{1,0:T(8,128)} %copy-done.15, ...), kind=kLoop, calls=%fused_computation.80 | loop fusion | flops 34603008 | bytes 25205008 | tf_op jit(solution)/shard_map/add | solution.py:34
  302.9 5.4 collective-permute-start.12
  310.2 18.1 %add_add_fusion.1 = f32[256,4096]{1,0:T(8,128)} fusion(f32[256,4096]{1,0:T(8,128)} %add_add_fusion.2, pred[256,4096]{1,0:T(8,128)(4,1)} %get-tuple-element.15, f32[1,4096]{1,0:T(1,128)S(1)} %collective-permute-done.24, f32[1,4096]{1,0:T(1,128)} %copy-done.23, pred[256,4096]{1,0:T(8,128)(4,1)} %get-tuple-element.14, f32[258,1]{1,0:T(8,128)S(1)} %collective-permute-done.26, ...), kind=kLoop, calls=%fused_computation.74 | loop fusion | flops 34603008 | bytes 25205008 | tf_op jit(solution)/shard_map/add | solution.py:34
  351.4 20.9 %multiply_bitcast_fusion = (f32[1,256,4096]{2,1,0:T(8,128)}, f32[256,4096]{1,0:T(8,128)}) fusion(f32[256,4096]{1,0:T(8,128)} %add_add_fusion.5, f32[256,4096]{1,0:T(8,128)S(1)} %get-tuple-element.8, f32[256,4096]{1,0:T(8,128)S(1)} %copy-done.2, bf16[1,4,64,4096]{3,2,1,0:T(8,128)(2,1)S(1)} %copy-done.6, f32[2,256,4096]{2,1,0:T(8,128)} %param.11, ...), kind=kLoop, calls=%fused_computation.78 | loop fusion | flops 38797312 | bytes 37787920 | tf_op jit(solution)/shard_map/stack | solution.py:76
  372.3 8.7 %copy.22 = f32[1,256,4096]{2,0,1:T(1,128)} copy(f32[1,256,4096]{2,1,0:T(8,128)} %get-tuple-element.6) | data formatting | bytes 8388608 | tf_op jit(solution)/shard_map/stack | solution.py:76
  381.1 19.5 %add_multiply_fusion = (f32[256,4096]{1,0:T(8,128)S(1)}, f32[256,4096]{1,0:T(8,128)}) fusion(f32[256,4096]{1,0:T(8,128)} %add_add_fusion.1, f32[256,4096]{1,0:T(8,128)S(1)} %copy-done.1, f32[256,4096]{1,0:T(8,128)} %add_add_fusion.2, bf16[1,4,64,4096]{3,2,1,0:T(8,128)(2,1)S(1)} %copy-done.4, f32[2,256,4096]{2,1,0:T(8,128)} %param.11, ...), kind=kLoop, calls=%fused_computation.72 | loop fusion | flops 38797312 | bytes 37787920 | tf_op jit(solution)/shard_map/add | solution.py:73
  405.2 9.2 %pad_maximum_fusion = f32[2,256,4096]{2,0,1:T(2,128)} fusion(f32[1,256,4096]{2,0,1:T(1,128)S(1)} %stack.19, f32[1,256,4096]{2,0,1:T(1,128)S(1)} %copy-done.11), kind=kLoop, calls=%fused_computation | loop fusion | flops 2097152 | bytes 16777216 | tf_op jit(solution)/shard_map/stack | solution.py:76
  414.4 6.8 %all-to-all-start.1 = ((f32[2,256,4096]{2,0,1:T(2,128)}), f32[2,256,4096]{2,0,1:T(2,128)}, u32[]{:S(2)}, u32[]{:S(2)}) async-start(f32[2,256,4096]{2,0,1:T(2,128)} %pad_maximum_fusion), calls=%async_computation.1 | async-start | bytes 16777216 | tf_op jit(solution)/shard_map/all_to_all | solution.py:76
  421.2 7.9 %pad_maximum_fusion.1 = f32[2,256,4096]{2,1,0:T(8,128)} fusion(f32[1,256,4096]{2,1,0:T(8,128)} %bitcast.143, f32[1,256,4096]{2,1,0:T(8,128)} %bitcast.142), kind=kLoop, calls=%fused_computation.1 | loop fusion | flops 2097152 | bytes 16777216 | tf_op jit(solution)/shard_map/stack | solution.py:77
  429.0 175.3 %all-to-all-done.1 = f32[2,256,4096]{2,0,1:T(2,128)} async-done(((f32[2,256,4096]{2,0,1:T(2,128)}), f32[2,256,4096]{2,0,1:T(2,128)}, u32[]{:S(2)}, u32[]{:S(2)}) %all-to-all-start.1) | async-done | bytes 8388640 | tf_op jit(solution)/shard_map/all_to_all | solution.py:76
  604.3 12.1 %copy.23 = f32[2,64,4,4096]{3,2,1,0:T(4,128)} copy(f32[2,64,4,4096]{3,0,1,2:T(2,128)} %bitcast.18) | data formatting | bytes 16777216 | tf_op jit(solution)/shard_map/all_to_all | solution.py:76
  616.4 10.9 %all_to_all.30 = f32[2,64,16384]{2,1,0:T(8,128)} reshape(f32[2,64,4,4096]{3,2,1,0:T(4,128)} %copy.23) | data formatting | bytes 16777216 | tf_op jit(solution)/shard_map/all_to_all | solution.py:76
  (152 shorter events, 106.4 us)
Async XLA Ops:
  28.0 97.7 %all-to-all-start = ((bf16[4,2,262144]{2,1,0:T(2,128)(2,1)}), bf16[4,2,262144]{2,1,0:T(2,128)(2,1)}, u32[]{:S(2)}, u32[]{:S(2)}) async-start(bf16[4,2,262144]{2,1,0:T(2,128)(2,1)} %reshape.44), calls=%async_computation | async-start | bytes 8388608 | tf_op jit(solution)/shard_map/all_to_all | solution.py:52
  34.1 16.3 %collective-permute-start = (f32[1,4096]{1,0:T(1,128)S(1)}, f32[1,4096]{1,0:T(1,128)S(1)}, u32[]{:S(2)}, u32[]{:S(2)}) collective-permute-start(f32[1,4096]{1,0:T(1,128)S(1)} %get-tuple-element.17), channel_id=1, source_target_pairs={{0,4},{4,8},{8,12},{12,16},{16,20},{20,24},{24,28},{1,5},{5,9},{9,... | collective-permute-start | bytes 49160 | tf_op jit(solution)/shard_map/ppermute | solution.py:16
  37.8 12.6 %collective-permute-start.1 = (f32[1,4096]{1,0:T(1,128)S(1)}, f32[1,4096]{1,0:T(1,128)S(1)}, u32[]{:S(2)}, u32[]{:S(2)}) collective-permute-start(f32[1,4096]{1,0:T(1,128)S(1)} %get-tuple-element.16), channel_id=1, source_target_pairs={{4,0},{8,4},{12,8},{16,12},{20,16},{24,20},{28,24},{5,1},{9,5},{13... | collective-permute-start | bytes 49160 | tf_op jit(solution)/shard_map/ppermute | solution.py:19
  39.7 15.8 %collective-permute-start.16 = (f32[1,4096]{1,0:T(1,128)S(1)}, f32[1,4096]{1,0:T(1,128)S(1)}, u32[]{:S(2)}, u32[]{:S(2)}) collective-permute-start(f32[1,4096]{1,0:T(1,128)S(1)} %get-tuple-element.19), channel_id=1, source_target_pairs={{0,4},{4,8},{8,12},{12,16},{16,20},{20,24},{24,28},{1,5},{5,9},{9,... | collective-permute-start | bytes 49160 | tf_op jit(solution)/shard_map/ppermute | solution.py:16
  50.5 107.2 %collective-permute-start.2 = (f32[258,1]{1,0:T(8,128)S(1)}, f32[258,1]{1,0:T(8,128)S(1)}, u32[]{:S(2)}, u32[]{:S(2)}) collective-permute-start(f32[258,1]{1,0:T(8,128)S(1)} %get-tuple-element.29), channel_id=1, source_target_pairs={{0,1},{1,2},{2,3},{4,5},{5,6},{6,7},{8,9},{9,10},{10,11},{12,13},{... | collective-permute-start | bytes 3104 | tf_op jit(solution)/shard_map/ppermute | solution.py:16
  54.2 103.5 %collective-permute-start.3 = (f32[258,1]{1,0:T(8,128)S(1)}, f32[258,1]{1,0:T(8,128)S(1)}, u32[]{:S(2)}, u32[]{:S(2)}) collective-permute-start(f32[258,1]{1,0:T(8,128)S(1)} %get-tuple-element.28), channel_id=1, source_target_pairs={{1,0},{2,1},{3,2},{5,4},{6,5},{7,6},{9,8},{10,9},{11,10},{13,12},{... | collective-permute-start | bytes 3104 | tf_op jit(solution)/shard_map/ppermute | solution.py:19
  55.7 130.4 %collective-permute-start.18 = (f32[258,1]{1,0:T(8,128)S(1)}, f32[258,1]{1,0:T(8,128)S(1)}, u32[]{:S(2)}, u32[]{:S(2)}) collective-permute-start(f32[258,1]{1,0:T(8,128)S(1)} %get-tuple-element.37), channel_id=1, source_target_pairs={{0,1},{1,2},{2,3},{4,5},{5,6},{6,7},{8,9},{9,10},{10,11},{12,13},{... | collective-permute-start | bytes 3104 | tf_op jit(solution)/shard_map/ppermute | solution.py:16
  59.7 126.4 %collective-permute-start.19 = (f32[258,1]{1,0:T(8,128)S(1)}, f32[258,1]{1,0:T(8,128)}, u32[]{:S(2)}, u32[]{:S(2)}) collective-permute-start(f32[258,1]{1,0:T(8,128)S(1)} %get-tuple-element.36), channel_id=1, source_target_pairs={{1,0},{2,1},{3,2},{5,4},{6,5},{7,6},{9,8},{10,9},{11,10},{13,12},{... | collective-permute-start | bytes 3104 | tf_op jit(solution)/shard_map/ppermute | solution.py:19
  178.5 33.7 %collective-permute-start.4 = (f32[1,4096]{1,0:T(1,128)S(1)}, f32[1,4096]{1,0:T(1,128)S(1)}, u32[]{:S(2)}, u32[]{:S(2)}) collective-permute-start(f32[1,4096]{1,0:T(1,128)S(1)} %get-tuple-element.43), channel_id=1, source_target_pairs={{0,4},{4,8},{8,12},{12,16},{16,20},{20,24},{24,28},{1,5},{5,9},{9,... | collective-permute-start | bytes 49160 | tf_op jit(solution)/shard_map/ppermute | solution.py:16
  184.1 28.1 %collective-permute-start.5 = (f32[1,4096]{1,0:T(1,128)S(1)}, f32[1,4096]{1,0:T(1,128)S(1)}, u32[]{:S(2)}, u32[]{:S(2)}) collective-permute-start(f32[1,4096]{1,0:T(1,128)S(1)} %get-tuple-element.42), channel_id=1, source_target_pairs={{4,0},{8,4},{12,8},{16,12},{20,16},{24,20},{28,24},{5,1},{9,5},{13... | collective-permute-start | bytes 49160 | tf_op jit(solution)/shard_map/ppermute | solution.py:19
  216.4 26.8 %collective-permute-start.22 = (f32[258,1]{1,0:T(8,128)S(1)}, f32[258,1]{1,0:T(8,128)S(1)}, u32[]{:S(2)}, u32[]{:S(2)}) collective-permute-start(f32[258,1]{1,0:T(8,128)S(1)} %get-tuple-element.35), channel_id=1, source_target_pairs={{0,1},{1,2},{2,3},{4,5},{5,6},{6,7},{8,9},{9,10},{10,11},{12,13},{... | collective-permute-start | bytes 3104 | tf_op jit(solution)/shard_map/ppermute | solution.py:16
  219.3 23.9 %collective-permute-start.23 = (f32[258,1]{1,0:T(8,128)S(1)}, f32[258,1]{1,0:T(8,128)}, u32[]{:S(2)}, u32[]{:S(2)}) collective-permute-start(f32[258,1]{1,0:T(8,128)S(1)} %get-tuple-element.34), channel_id=1, source_target_pairs={{1,0},{2,1},{3,2},{5,4},{6,5},{7,6},{9,8},{10,9},{11,10},{13,12},{... | collective-permute-start | bytes 3104 | tf_op jit(solution)/shard_map/ppermute | solution.py:19
  236.2 32.9 %collective-permute-start.8 = (f32[1,4096]{1,0:T(1,128)}, f32[1,4096]{1,0:T(1,128)S(1)}, u32[]{:S(2)}, u32[]{:S(2)}) collective-permute-start(f32[1,4096]{1,0:T(1,128)} %get-tuple-element.41), channel_id=1, source_target_pairs={{0,4},{4,8},{8,12},{12,16},{16,20},{20,24},{24,28},{1,5},{5,9},{9,... | collective-permute-start | bytes 49160 | tf_op jit(solution)/shard_map/ppermute | solution.py:16
  241.3 27.8 %collective-permute-start.9 = (f32[1,4096]{1,0:T(1,128)}, f32[1,4096]{1,0:T(1,128)S(1)}, u32[]{:S(2)}, u32[]{:S(2)}) collective-permute-start(f32[1,4096]{1,0:T(1,128)} %get-tuple-element.40), channel_id=1, source_target_pairs={{4,0},{8,4},{12,8},{16,12},{20,16},{24,20},{28,24},{5,1},{9,5},{13... | collective-permute-start | bytes 49160 | tf_op jit(solution)/shard_map/ppermute | solution.py:19
  262.4 13.3 %collective-permute-start.24 = (f32[1,4096]{1,0:T(1,128)S(1)}, f32[1,4096]{1,0:T(1,128)S(1)}, u32[]{:S(2)}, u32[]{:S(2)}) collective-permute-start(f32[1,4096]{1,0:T(1,128)S(1)} %get-tuple-element.49), channel_id=1, source_target_pairs={{0,4},{4,8},{8,12},{12,16},{16,20},{20,24},{24,28},{1,5},{5,9},{9,... | collective-permute-start | bytes 49160 | tf_op jit(solution)/shard_map/ppermute | solution.py:16
  276.3 33.9 %collective-permute-start.26 = (f32[258,1]{1,0:T(8,128)S(1)}, f32[258,1]{1,0:T(8,128)S(1)}, u32[]{:S(2)}, u32[]{:S(2)}) collective-permute-start(f32[258,1]{1,0:T(8,128)S(1)} %get-tuple-element.33), channel_id=1, source_target_pairs={{0,1},{1,2},{2,3},{4,5},{5,6},{6,7},{8,9},{9,10},{10,11},{12,13},{... | collective-permute-start | bytes 3104 | tf_op jit(solution)/shard_map/ppermute | solution.py:16
  280.3 29.9 %collective-permute-start.27 = (f32[258,1]{1,0:T(8,128)S(1)}, f32[258,1]{1,0:T(8,128)}, u32[]{:S(2)}, u32[]{:S(2)}) collective-permute-start(f32[258,1]{1,0:T(8,128)S(1)} %get-tuple-element.32), channel_id=1, source_target_pairs={{1,0},{2,1},{3,2},{5,4},{6,5},{7,6},{9,8},{10,9},{11,10},{13,12},{... | collective-permute-start | bytes 3104 | tf_op jit(solution)/shard_map/ppermute | solution.py:19
  302.9 33.3 %collective-permute-start.12 = (f32[1,4096]{1,0:T(1,128)}, f32[1,4096]{1,0:T(1,128)S(1)}, u32[]{:S(2)}, u32[]{:S(2)}) collective-permute-start(f32[1,4096]{1,0:T(1,128)} %get-tuple-element.38), channel_id=1, source_target_pairs={{0,4},{4,8},{8,12},{12,16},{16,20},{20,24},{24,28},{1,5},{5,9},{9,... | collective-permute-start | bytes 49160 | tf_op jit(solution)/shard_map/ppermute | solution.py:16
  308.3 28.0 %collective-permute-start.13 = (f32[1,4096]{1,0:T(1,128)S(1)}, f32[1,4096]{1,0:T(1,128)S(1)}, u32[]{:S(2)}, u32[]{:S(2)}) collective-permute-start(f32[1,4096]{1,0:T(1,128)S(1)} %get-tuple-element.39), channel_id=1, source_target_pairs={{4,0},{8,4},{12,8},{16,12},{20,16},{24,20},{28,24},{5,1},{9,5},{13... | collective-permute-start | bytes 49160 | tf_op jit(solution)/shard_map/ppermute | solution.py:19
  329.3 13.7 %collective-permute-start.28 = (f32[1,4096]{1,0:T(1,128)S(1)}, f32[1,4096]{1,0:T(1,128)S(1)}, u32[]{:S(2)}, u32[]{:S(2)}) collective-permute-start(f32[1,4096]{1,0:T(1,128)S(1)} %get-tuple-element.46), channel_id=1, source_target_pairs={{0,4},{4,8},{8,12},{12,16},{16,20},{20,24},{24,28},{1,5},{5,9},{9,... | collective-permute-start | bytes 49160 | tf_op jit(solution)/shard_map/ppermute | solution.py:16
  337.4 13.9 %collective-permute-start.14 = (f32[258,1]{1,0:T(8,128)S(1)}, f32[258,1]{1,0:T(8,128)S(1)}, u32[]{:S(2)}, u32[]{:S(2)}) collective-permute-start(f32[258,1]{1,0:T(8,128)S(1)} %get-tuple-element.22), channel_id=1, source_target_pairs={{0,1},{1,2},{2,3},{4,5},{5,6},{6,7},{8,9},{9,10},{10,11},{12,13},{... | collective-permute-start | bytes 3104 | tf_op jit(solution)/shard_map/ppermute | solution.py:16
  344.8 36.2 %collective-permute-start.30 = (f32[258,1]{1,0:T(8,128)}, f32[258,1]{1,0:T(8,128)S(1)}, u32[]{:S(2)}, u32[]{:S(2)}) collective-permute-start(f32[258,1]{1,0:T(8,128)} %get-tuple-element.30), channel_id=1, source_target_pairs={{0,1},{1,2},{2,3},{4,5},{5,6},{6,7},{8,9},{9,10},{10,11},{12,13},{... | collective-permute-start | bytes 3104 | tf_op jit(solution)/shard_map/ppermute | solution.py:16
  349.6 31.4 %collective-permute-start.31 = (f32[258,1]{1,0:T(8,128)S(1)}, f32[258,1]{1,0:T(8,128)S(1)}, u32[]{:S(2)}, u32[]{:S(2)}) collective-permute-start(f32[258,1]{1,0:T(8,128)S(1)} %get-tuple-element.31), channel_id=1, source_target_pairs={{1,0},{2,1},{3,2},{5,4},{6,5},{7,6},{9,8},{10,9},{11,10},{13,12},{... | collective-permute-start | bytes 3104 | tf_op jit(solution)/shard_map/ppermute | solution.py:19
  414.4 189.9 %all-to-all-start.1 = ((f32[2,256,4096]{2,0,1:T(2,128)}), f32[2,256,4096]{2,0,1:T(2,128)}, u32[]{:S(2)}, u32[]{:S(2)}) async-start(f32[2,256,4096]{2,0,1:T(2,128)} %pad_maximum_fusion), calls=%async_computation.1 | async-start | bytes 16777216 | tf_op jit(solution)/shard_map/all_to_all | solution.py:76
  (44 other events, 794.5 us)
where the time goes:
time: 638 us; the launch traced here: 628 us
  waiting for transfers between devices  242 us (38%)
  other arithmetic  169 us (26%)
  local copies, waits for them, and re-layouts  109 us (17%)
  starting transfers between devices  106 us (17%)
    all_to_all x1, waiting for transfers between devices, body(): lax.all_to_all(jnp.stack(phases), 'cols', split_axis=1, concat_axis=2, ti...  175 us
    add x6, other arithmetic, advance(): middle - jnp.abs(wind_x) * (middle - upwind_x)  107 us
    ppermute x16, starting transfers between devices, extended(): lax.ppermute(lax.slice_in_dim(block, block.shape[dim] - width, None, axis...  67.2 us
    all_to_all x1, waiting for transfers between devices, body(): lax.all_to_all(irradiance_layers, 'cols', split_axis=2, concat_axis=1, ti...  64.7 us
    unnamed x71, local copies, waits for them, and re-layouts  39.5 us
    another operation x2, other arithmetic, body(): jnp.stack(phases)  30.1 us
    ppermute x16, starting transfers between devices, extended(): lax.ppermute(lax.slice_in_dim(block, 0, width, axis=dim), axis, backward)  26.7 us
    all_to_all x2, local copies, waits for them, and re-layouts, body(): lax.all_to_all(jnp.stack(phases), 'cols', split_axis=1, concat_axis=2, ti...  23 us
  transfers between devices with their start and end apart: 34, of which 4 were waited for; matrix products, arithmetic and copies ran while one was open for 31% of the time, Pallas kernels for 0%

commit v1 on v0

--- a/solution.py
+++ b/solution.py
@@ -6,6 +6,17 @@
 SUBSTEPS = 4
 DIFFUSION = 0.03
 HEAT_RATE = 0.25
+
+
+def in_blocks(x, dim, count):
+    before, after = (x.shape[:dim], x.shape[dim + 1 :])
+    return jnp.moveaxis(x.reshape(*before, count, -1, *after), dim, 0)
+
+
+def joined_along(tiles, dim):
+    dims = list(tiles.shape[1:])
+    dims[dim] *= tiles.shape[0]
+    return jnp.moveaxis(tiles, 0, dim).reshape(dims)
 
 
 def extended(block, sides, width):
@@ -73,7 +84,15 @@
             phase_sum = phase_sum + heat_transport_advance / SUBSTEPS
         phases.append(phase_sum)
         finals.append(heat_transport_advance)
-    phase_slabs = lax.all_to_all(jnp.stack(phases), "cols", split_axis=1, concat_axis=2, tiled=True)
+    value = jnp.stack(phases)
+    size, here = (lax.axis_size("cols"), lax.axis_index("cols"))
+    blocks = in_blocks(value, 1, size)
+    outs = [blocks[here]]
+    for step in range(1, size):
+        sent = blocks[here ^ step]
+        outs.append(lax.ppermute(sent, "cols", [(i_2, i_2 ^ step) for i_2 in range(size)]))
+    blocks = jnp.stack(outs)[here ^ jnp.arange(size)]
+    phase_slabs = joined_along(blocks, 2)
     return (phase_slabs, jnp.stack(finals))
 
 

time: 638 us -> 612 us (0.959)
  the two profiles are of different devices: /device:TPU:3 before, /device:TPU:19 now
where the time goes in v1:
time: 612 us; the launch traced here: 601 us
  waiting for transfers between devices  232 us (38%)
  other arithmetic  166 us (27%)
  starting transfers between devices  109 us (18%)
  local copies, waits for them, and re-layouts  92.2 us (15%)
    ppermute x3, waiting for transfers between devices, body(): lax.ppermute(sent, 'cols', [(i_2, i_2 ^ step) for i_2 in range(size)])  176 us
    add x6, other arithmetic, advance(): middle - jnp.abs(wind_x) * (middle - upwind_x)  107 us
    ppermute x16, starting transfers between devices, extended(): lax.ppermute(lax.slice_in_dim(block, block.shape[dim] - width, None, axis...  69 us
    all_to_all x1, waiting for transfers between devices, body(): lax.all_to_all(irradiance_layers, 'cols', split_axis=2, concat_axis=1, ti...  55.9 us
    add x2, other arithmetic, body(): phase_sum = phase_sum + heat_transport_advance / SUBSTEPS  42.2 us
    unnamed x59, local copies, waits for them, and re-layouts  39.3 us
    ppermute x16, starting transfers between devices, extended(): lax.ppermute(lax.slice_in_dim(block, 0, width, axis=dim), axis, backward)  32.2 us
    all_to_all x1, local copies, waits for them, and re-layouts, body(): lax.all_to_all(irradiance_layers, 'cols', split_axis=2, concat_axis=1, ti...  18.6 us
  transfers between devices with their start and end apart: 36, of which 4 were waited for; matrix products, arithmetic and copies ran while one was open for 31% of the time, Pallas kernels for 0%

profile of v1, /device:TPU:19, one launch (start us, length us, event | category | flops | bytes accessed | tf_op | source)
XLA Modules:
  0.0 601.3 jit_solution(9972487017976849196)
XLA Ops:
  0.6 17.8 %copy.27 = bf16[2,64,16384]{1,0,2:T(2,128)(2,1)} copy(bf16[2,64,16384]{2,1,0:T(8,128)(2,1)} %param.7) | data formatting | bytes 8388608 | tf_op args[0]
  18.4 9.6 %reshape.84 = bf16[4,2,262144]{2,1,0:T(2,128)(2,1)} reshape(bf16[16384,2,64]{2,1,0:T(2,128)(2,1)} %bitcast.160) | data formatting | bytes 8388608
  28.0 5.0 all-to-all-start
  46.7 7.8 %slice_bitcast_fusion = (f32[256,4096]{1,0:T(8,128)}, f32[256,4096]{1,0:T(8,128)}) fusion(f32[2,256,4096]{2,1,0:T(8,128)} %param.8), kind=kLoop, calls=%fused_computation.86 | loop fusion | bytes 16777216 | tf_op jit(solution)/shard_map/squeeze | solution.py:79
  66.7 55.9 %all-to-all-done = bf16[4,2,262144]{2,1,0:T(2,128)(2,1)} async-done(((bf16[4,2,262144]{2,1,0:T(2,128)(2,1)}), bf16[4,2,262144]{2,1,0:T(2,128)(2,1)}, u32[]{:S(2)}, u32[]{:S(2)}) %all-to-all-start) | async-done | bytes 4194336 | tf_op jit(solution)/shard_map/all_to_all | solution.py:63
  122.6 9.3 %reshape.85 = bf16[16384,2,64]{2,1,0:T(2,128)(2,1)} reshape(bf16[4,2,262144]{2,1,0:T(2,128)(2,1)} %all-to-all-done) | data formatting | bytes 8388608
  131.8 18.6 %copy.29 = bf16[2,64,4,4096]{3,1,2,0:T(8,128)(2,1)} copy(bf16[2,64,4,4096]{1,0,3,2:T(2,128)(2,1)} %bitcast.159) | data formatting | bytes 8388608 | tf_op jit(solution)/shard_map/all_to_all | solution.py:63
  155.3 20.9 %add_add_fusion.3 = (f32[256,4096]{1,0:T(8,128)S(1)}, pred[256,4096]{1,0:T(8,128)(4,1)}, pred[256,4096]{1,0:T(8,128)(4,1)}) fusion(f32[256,4096]{1,0:T(8,128)} %get-tuple-element.24, f32[1,4096]{1,0:T(1,128)S(1)} %collective-permute-done.16, f32[1,4096]{1,0:T(1,128)S(1)} %collective-permute-done.17, f32[258,1]{1,0:T(8,128)} %copy-done.11, ...), kind=kLoop, calls=%fused_computation.85 | loop fusion | flops 36700160 | bytes 25205008 | tf_op jit(solution)/shard_map/add | solution.py:45
  176.2 5.7 collective-permute-start.20
  183.9 18.8 %add_add_fusion.7 = (f32[256,4096]{1,0:T(8,128)S(1)}, pred[256,4096]{1,0:T(8,128)(4,1)}, pred[256,4096]{1,0:T(8,128)(4,1)}) fusion(f32[256,4096]{1,0:T(8,128)} %get-tuple-element.25, f32[1,4096]{1,0:T(1,128)S(1)} %collective-permute-done, f32[1,4096]{1,0:T(1,128)S(1)} %collective-permute-done.1, f32[258,1]{1,0:T(8,128)S(1)} %collective-permute-done.2, ...), kind=kLoop, calls=%fused_computation.91 | loop fusion | flops 36700160 | bytes 25205008 | tf_op jit(solution)/shard_map/add | solution.py:45
  222.7 12.5 %add_add_fusion.2 = f32[256,4096]{1,0:T(8,128)} fusion(f32[256,4096]{1,0:T(8,128)S(1)} %get-tuple-element.8, pred[256,4096]{1,0:T(8,128)(4,1)} %get-tuple-element.10, f32[1,4096]{1,0:T(1,128)S(1)} %collective-permute-done.20, f32[1,4096]{1,0:T(1,128)S(1)} %collective-permute-done.21, pred[256,4096]{1,0:T(8,128)(4,1)} %get-tuple-element.9, ...), kind=kLoop, calls=%fused_computation.84 | loop fusion | flops 34603008 | bytes 25205008 | tf_op jit(solution)/shard_map/add | solution.py:45
  236.8 5.4 collective-permute-start.24
  244.1 18.0 %add_add_fusion.6 = f32[256,4096]{1,0:T(8,128)} fusion(f32[256,4096]{1,0:T(8,128)} %copy-done, pred[256,4096]{1,0:T(8,128)(4,1)} %get-tuple-element.15, f32[1,4096]{1,0:T(1,128)S(1)} %collective-permute-done.4, f32[1,4096]{1,0:T(1,128)} %copy-done.16, pred[256,4096]{1,0:T(8,128)(4,1)} %get-tuple-element.14, f32[258,1]{1,0:T(8,128)S(1)} %collective-permute-done.6, ...), kind=kLoop, calls=%fused_computation.90 | loop fusion | flops 34603008 | bytes 25205008 | tf_op jit(solution)/shard_map/add | solution.py:45
  284.2 18.9 %add_add_fusion.1 = f32[256,4096]{1,0:T(8,128)} fusion(f32[256,4096]{1,0:T(8,128)} %add_add_fusion.2, pred[256,4096]{1,0:T(8,128)(4,1)} %get-tuple-element.10, f32[1,4096]{1,0:T(1,128)S(1)} %collective-permute-done.24, f32[1,4096]{1,0:T(1,128)S(1)} %collective-permute-done.25, pred[256,4096]{1,0:T(8,128)(4,1)} %get-tuple-element.9, f32[258,1]{1,0:T(8,128)} %copy-done.14, ...), kind=kLoop, calls=%fused_computation.83 | loop fusion | flops 34603008 | bytes 25205008 | tf_op jit(solution)/shard_map/add | solution.py:45
  304.8 5.4 collective-permute-start.28
  312.1 18.1 %add_add_fusion.5 = f32[256,4096]{1,0:T(8,128)} fusion(f32[256,4096]{1,0:T(8,128)} %add_add_fusion.6, pred[256,4096]{1,0:T(8,128)(4,1)} %get-tuple-element.15, f32[1,4096]{1,0:T(1,128)S(1)} %collective-permute-done.8, f32[1,4096]{1,0:T(1,128)} %copy-done.17, pred[256,4096]{1,0:T(8,128)(4,1)} %get-tuple-element.14, f32[258,1]{1,0:T(8,128)S(1)} %collective-permute-done.10, ...), kind=kLoop, calls=%fused_computation.89 | loop fusion | flops 34603008 | bytes 25205008 | tf_op jit(solution)/shard_map/add | solution.py:45
  352.2 21.0 %add_multiply_fusion = (f32[256,4096]{1,0:T(8,128)}, f32[256,4096]{1,0:T(8,128)}) fusion(f32[256,4096]{1,0:T(8,128)} %add_add_fusion.1, f32[256,4096]{1,0:T(8,128)S(1)} %get-tuple-element.8, f32[256,4096]{1,0:T(8,128)} %add_add_fusion.2, bf16[1,4,64,4096]{3,2,1,0:T(8,128)(2,1)} %copy-done.4, f32[2,256,4096]{2,1,0:T(8,128)} %param.11, ...), kind=kLoop, calls=%fused_computation.81 | loop fusion | flops 38797312 | bytes 37787920 | tf_op jit(solution)/shard_map/add | solution.py:84
  373.3 21.2 %add_multiply_fusion.1 = (f32[256,4096]{1,0:T(8,128)}, f32[256,4096]{1,0:T(8,128)}) fusion(f32[256,4096]{1,0:T(8,128)} %add_add_fusion.5, f32[256,4096]{1,0:T(8,128)S(1)} %copy-done.1, f32[256,4096]{1,0:T(8,128)} %add_add_fusion.6, bf16[1,4,64,4096]{3,2,1,0:T(8,128)(2,1)S(1)} %copy-done.3, f32[2,256,4096]{2,1,0:T(8,128)S(1)} %bitcast.155, ...), kind=kLoop, calls=%fused_computation.87 | loop fusion | flops 38797312 | bytes 37787920 | tf_op jit(solution)/shard_map/add | solution.py:84
  404.2 81.9 %collective-permute-done.32 = f32[2,64,4096]{2,1,0:T(8,128)S(1)} collective-permute-done((f32[2,64,4096]{2,1,0:T(8,128)S(1)}, f32[2,64,4096]{2,1,0:T(8,128)S(1)}, u32[]{:S(2)}, u32[]{:S(2)}) %collective-permute-start.32) | collective-permute-done | bytes 2097184 | tf_op jit(solution)/shard_map/ppermute | solution.py:93
  486.0 47.9 %collective-permute-done.33 = f32[2,64,4096]{2,1,0:T(8,128)S(1)} collective-permute-done((f32[2,64,4096]{2,1,0:T(8,128)S(1)}, f32[2,64,4096]{2,1,0:T(8,128)S(1)}, u32[]{:S(2)}, u32[]{:S(2)}) %collective-permute-start.33) | collective-permute-done | bytes 2097184 | tf_op jit(solution)/shard_map/ppermute | solution.py:93
  533.9 46.6 %collective-permute-done.34 = f32[2,64,4096]{2,1,0:T(8,128)} collective-permute-done((f32[2,64,4096]{2,1,0:T(8,128)S(1)}, f32[2,64,4096]{2,1,0:T(8,128)}, u32[]{:S(2)}, u32[]{:S(2)}) %collective-permute-start.34) | collective-permute-done | bytes 2097184 | tf_op jit(solution)/shard_map/ppermute | solution.py:93
  580.5 4.9 pad_maximum_fusion
  585.4 7.8 %gather_fusion = f32[4,2,64,4096]{3,2,1,0:T(8,128)} fusion(f32[4,2,64,4096]{3,2,1,0:T(8,128)} %pad_maximum_fusion, s32[1024]{0:T(1024)S(1)} %pad_clamp_fusion), kind=kCustom, calls=%fused_computation | custom fusion | bytes 16777232 | tf_op jit(solution)/shard_map/gather | solution.py:94
  593.3 7.8 %copy.35 = f32[4,2,8,8,4096]{4,3,0,2,1:T(8,128)} copy(f32[4,2,8,8,4096]{4,3,2,1,0:T(8,128)} %bitcast.158) | data formatting | bytes 16777216 | tf_op jit(solution)/shard_map/reshape | solution.py:19
  (146 shorter events, 112.7 us)
Async XLA Ops:
  28.0 94.6 %all-to-all-start = ((bf16[4,2,262144]{2,1,0:T(2,128)(2,1)}), bf16[4,2,262144]{2,1,0:T(2,128)(2,1)}, u32[]{:S(2)}, u32[]{:S(2)}) async-start(bf16[4,2,262144]{2,1,0:T(2,128)(2,1)} %reshape.84), calls=%async_computation | async-start | bytes 8388608 | tf_op jit(solution)/shard_map/all_to_all | solution.py:63
  34.2 20.4 %collective-permute-start.16 = (f32[1,4096]{1,0:T(1,128)S(1)}, f32[1,4096]{1,0:T(1,128)S(1)}, u32[]{:S(2)}, u32[]{:S(2)}) collective-permute-start(f32[1,4096]{1,0:T(1,128)S(1)} %get-tuple-element.23), channel_id=1, source_target_pairs={{0,4},{4,8},{8,12},{12,16},{16,20},{20,24},{24,28},{1,5},{5,9},{9,... | collective-permute-start | bytes 49160 | tf_op jit(solution)/shard_map/ppermute | solution.py:27
  38.1 16.5 %collective-permute-start.17 = (f32[1,4096]{1,0:T(1,128)S(1)}, f32[1,4096]{1,0:T(1,128)S(1)}, u32[]{:S(2)}, u32[]{:S(2)}) collective-permute-start(f32[1,4096]{1,0:T(1,128)S(1)} %get-tuple-element.20), channel_id=1, source_target_pairs={{4,0},{8,4},{12,8},{16,12},{20,16},{24,20},{28,24},{5,1},{9,5},{13... | collective-permute-start | bytes 49160 | tf_op jit(solution)/shard_map/ppermute | solution.py:30
  40.0 21.2 %collective-permute-start = (f32[1,4096]{1,0:T(1,128)S(1)}, f32[1,4096]{1,0:T(1,128)S(1)}, u32[]{:S(2)}, u32[]{:S(2)}) collective-permute-start(f32[1,4096]{1,0:T(1,128)S(1)} %get-tuple-element.22), channel_id=1, source_target_pairs={{0,4},{4,8},{8,12},{12,16},{16,20},{20,24},{24,28},{1,5},{5,9},{9,... | collective-permute-start | bytes 49160 | tf_op jit(solution)/shard_map/ppermute | solution.py:27
  44.6 16.7 %collective-permute-start.1 = (f32[1,4096]{1,0:T(1,128)S(1)}, f32[1,4096]{1,0:T(1,128)S(1)}, u32[]{:S(2)}, u32[]{:S(2)}) collective-permute-start(f32[1,4096]{1,0:T(1,128)S(1)} %get-tuple-element.21), channel_id=1, source_target_pairs={{4,0},{8,4},{12,8},{16,12},{20,16},{24,20},{28,24},{5,1},{9,5},{13... | collective-permute-start | bytes 49160 | tf_op jit(solution)/shard_map/ppermute | solution.py:30
  55.8 98.7 %collective-permute-start.18 = (f32[258,1]{1,0:T(8,128)S(1)}, f32[258,1]{1,0:T(8,128)S(1)}, u32[]{:S(2)}, u32[]{:S(2)}) collective-permute-start(f32[258,1]{1,0:T(8,128)S(1)} %get-tuple-element.33), channel_id=1, source_target_pairs={{0,1},{1,2},{2,3},{4,5},{5,6},{6,7},{8,9},{9,10},{10,11},{12,13},{... | collective-permute-start | bytes 3104 | tf_op jit(solution)/shard_map/ppermute | solution.py:27
  59.0 95.5 %collective-permute-start.19 = (f32[258,1]{1,0:T(8,128)S(1)}, f32[258,1]{1,0:T(8,128)S(1)}, u32[]{:S(2)}, u32[]{:S(2)}) collective-permute-start(f32[258,1]{1,0:T(8,128)S(1)} %get-tuple-element.32), channel_id=1, source_target_pairs={{1,0},{2,1},{3,2},{5,4},{6,5},{7,6},{9,8},{10,9},{11,10},{13,12},{... | collective-permute-start | bytes 3104 | tf_op jit(solution)/shard_map/ppermute | solution.py:30
  61.4 122.4 %collective-permute-start.2 = (f32[258,1]{1,0:T(8,128)S(1)}, f32[258,1]{1,0:T(8,128)S(1)}, u32[]{:S(2)}, u32[]{:S(2)}) collective-permute-start(f32[258,1]{1,0:T(8,128)S(1)} %get-tuple-element.41), channel_id=1, source_target_pairs={{0,1},{1,2},{2,3},{4,5},{5,6},{6,7},{8,9},{9,10},{10,11},{12,13},{... | collective-permute-start | bytes 3104 | tf_op jit(solution)/shard_map/ppermute | solution.py:27
  64.5 119.3 %collective-permute-start.3 = (f32[258,1]{1,0:T(8,128)S(1)}, f32[258,1]{1,0:T(8,128)}, u32[]{:S(2)}, u32[]{:S(2)}) collective-permute-start(f32[258,1]{1,0:T(8,128)S(1)} %get-tuple-element.40), channel_id=1, source_target_pairs={{1,0},{2,1},{3,2},{5,4},{6,5},{7,6},{9,8},{10,9},{11,10},{13,12},{... | collective-permute-start | bytes 3104 | tf_op jit(solution)/shard_map/ppermute | solution.py:30
  176.2 33.0 %collective-permute-start.20 = (f32[1,4096]{1,0:T(1,128)S(1)}, f32[1,4096]{1,0:T(1,128)S(1)}, u32[]{:S(2)}, u32[]{:S(2)}) collective-permute-start(f32[1,4096]{1,0:T(1,128)S(1)} %get-tuple-element.47), channel_id=1, source_target_pairs={{0,4},{4,8},{8,12},{12,16},{16,20},{20,24},{24,28},{1,5},{5,9},{9,... | collective-permute-start | bytes 49160 | tf_op jit(solution)/shard_map/ppermute | solution.py:27
  181.9 27.4 %collective-permute-start.21 = (f32[1,4096]{1,0:T(1,128)S(1)}, f32[1,4096]{1,0:T(1,128)S(1)}, u32[]{:S(2)}, u32[]{:S(2)}) collective-permute-start(f32[1,4096]{1,0:T(1,128)S(1)} %get-tuple-element.46), channel_id=1, source_target_pairs={{4,0},{8,4},{12,8},{16,12},{20,16},{24,20},{28,24},{5,1},{9,5},{13... | collective-permute-start | bytes 49160 | tf_op jit(solution)/shard_map/ppermute | solution.py:30
  215.6 28.5 %collective-permute-start.6 = (f32[258,1]{1,0:T(8,128)S(1)}, f32[258,1]{1,0:T(8,128)S(1)}, u32[]{:S(2)}, u32[]{:S(2)}) collective-permute-start(f32[258,1]{1,0:T(8,128)S(1)} %get-tuple-element.39), channel_id=1, source_target_pairs={{0,1},{1,2},{2,3},{4,5},{5,6},{6,7},{8,9},{9,10},{10,11},{12,13},{... | collective-permute-start | bytes 3104 | tf_op jit(solution)/shard_map/ppermute | solution.py:27
  219.5 24.7 %collective-permute-start.7 = (f32[258,1]{1,0:T(8,128)S(1)}, f32[258,1]{1,0:T(8,128)}, u32[]{:S(2)}, u32[]{:S(2)}) collective-permute-start(f32[258,1]{1,0:T(8,128)S(1)} %get-tuple-element.38), channel_id=1, source_target_pairs={{1,0},{2,1},{3,2},{5,4},{6,5},{7,6},{9,8},{10,9},{11,10},{13,12},{... | collective-permute-start | bytes 3104 | tf_op jit(solution)/shard_map/ppermute | solution.py:30
  236.8 33.1 %collective-permute-start.24 = (f32[1,4096]{1,0:T(1,128)}, f32[1,4096]{1,0:T(1,128)S(1)}, u32[]{:S(2)}, u32[]{:S(2)}) collective-permute-start(f32[1,4096]{1,0:T(1,128)} %get-tuple-element.45), channel_id=1, source_target_pairs={{0,4},{4,8},{8,12},{12,16},{16,20},{20,24},{24,28},{1,5},{5,9},{9,... | collective-permute-start | bytes 49160 | tf_op jit(solution)/shard_map/ppermute | solution.py:27
  242.2 27.8 %collective-permute-start.25 = (f32[1,4096]{1,0:T(1,128)}, f32[1,4096]{1,0:T(1,128)S(1)}, u32[]{:S(2)}, u32[]{:S(2)}) collective-permute-start(f32[1,4096]{1,0:T(1,128)} %get-tuple-element.44), channel_id=1, source_target_pairs={{4,0},{8,4},{12,8},{16,12},{20,16},{24,20},{28,24},{5,1},{9,5},{13... | collective-permute-start | bytes 49160 | tf_op jit(solution)/shard_map/ppermute | solution.py:30
  277.4 34.6 %collective-permute-start.10 = (f32[258,1]{1,0:T(8,128)S(1)}, f32[258,1]{1,0:T(8,128)S(1)}, u32[]{:S(2)}, u32[]{:S(2)}) collective-permute-start(f32[258,1]{1,0:T(8,128)S(1)} %get-tuple-element.37), channel_id=1, source_target_pairs={{0,1},{1,2},{2,3},{4,5},{5,6},{6,7},{8,9},{9,10},{10,11},{12,13},{... | collective-permute-start | bytes 3104 | tf_op jit(solution)/shard_map/ppermute | solution.py:27
  281.4 30.6 %collective-permute-start.11 = (f32[258,1]{1,0:T(8,128)S(1)}, f32[258,1]{1,0:T(8,128)}, u32[]{:S(2)}, u32[]{:S(2)}) collective-permute-start(f32[258,1]{1,0:T(8,128)S(1)} %get-tuple-element.36), channel_id=1, source_target_pairs={{1,0},{2,1},{3,2},{5,4},{6,5},{7,6},{9,8},{10,9},{11,10},{13,12},{... | collective-permute-start | bytes 3104 | tf_op jit(solution)/shard_map/ppermute | solution.py:30
  304.8 33.4 %collective-permute-start.28 = (f32[1,4096]{1,0:T(1,128)}, f32[1,4096]{1,0:T(1,128)S(1)}, u32[]{:S(2)}, u32[]{:S(2)}) collective-permute-start(f32[1,4096]{1,0:T(1,128)} %get-tuple-element.42), channel_id=1, source_target_pairs={{0,4},{4,8},{8,12},{12,16},{16,20},{20,24},{24,28},{1,5},{5,9},{9,... | collective-permute-start | bytes 49160 | tf_op jit(solution)/shard_map/ppermute | solution.py:27
  310.1 28.0 %collective-permute-start.29 = (f32[1,4096]{1,0:T(1,128)}, f32[1,4096]{1,0:T(1,128)S(1)}, u32[]{:S(2)}, u32[]{:S(2)}) collective-permute-start(f32[1,4096]{1,0:T(1,128)} %get-tuple-element.43), channel_id=1, source_target_pairs={{4,0},{8,4},{12,8},{16,12},{20,16},{24,20},{28,24},{5,1},{9,5},{13... | collective-permute-start | bytes 49160 | tf_op jit(solution)/shard_map/ppermute | solution.py:30
  346.3 27.0 %collective-permute-start.14 = (f32[258,1]{1,0:T(8,128)}, f32[258,1]{1,0:T(8,128)S(1)}, u32[]{:S(2)}, u32[]{:S(2)}) collective-permute-start(f32[258,1]{1,0:T(8,128)} %get-tuple-element.34), channel_id=1, source_target_pairs={{0,1},{1,2},{2,3},{4,5},{5,6},{6,7},{8,9},{9,10},{10,11},{12,13},{... | collective-permute-start | bytes 3104 | tf_op jit(solution)/shard_map/ppermute | solution.py:27
  349.7 23.6 %collective-permute-start.15 = (f32[258,1]{1,0:T(8,128)}, f32[258,1]{1,0:T(8,128)S(1)}, u32[]{:S(2)}, u32[]{:S(2)}) collective-permute-start(f32[258,1]{1,0:T(8,128)} %get-tuple-element.35), channel_id=1, source_target_pairs={{1,0},{2,1},{3,2},{5,4},{6,5},{7,6},{9,8},{10,9},{11,10},{13,12},{... | collective-permute-start | bytes 3104 | tf_op jit(solution)/shard_map/ppermute | solution.py:30
  397.5 88.6 %collective-permute-start.32 = (f32[2,64,4096]{2,1,0:T(8,128)S(1)}, f32[2,64,4096]{2,1,0:T(8,128)S(1)}, u32[]{:S(2)}, u32[]{:S(2)}) collective-permute-start(f32[2,64,4096]{2,1,0:T(8,128)S(1)} %get-tuple-element.17), channel_id=1, source_target_pairs={{0,1},{1,0},{2,3},{3,2},{4,5},{5,4},{6,7},{7,6},{8,9},{9,8},{10,11... | collective-permute-start | bytes 6291464 | tf_op jit(solution)/shard_map/ppermute | solution.py:93
  398.1 135.8 %collective-permute-start.33 = (f32[2,64,4096]{2,1,0:T(8,128)S(1)}, f32[2,64,4096]{2,1,0:T(8,128)S(1)}, u32[]{:S(2)}, u32[]{:S(2)}) collective-permute-start(f32[2,64,4096]{2,1,0:T(8,128)S(1)} %get-tuple-element.18), channel_id=1, source_target_pairs={{0,2},{1,3},{2,0},{3,1},{4,6},{5,7},{6,4},{7,5},{8,10},{9,11},{10,... | collective-permute-start | bytes 6291464 | tf_op jit(solution)/shard_map/ppermute | solution.py:93
  398.7 181.8 %collective-permute-start.34 = (f32[2,64,4096]{2,1,0:T(8,128)S(1)}, f32[2,64,4096]{2,1,0:T(8,128)}, u32[]{:S(2)}, u32[]{:S(2)}) collective-permute-start(f32[2,64,4096]{2,1,0:T(8,128)S(1)} %get-tuple-element.19), channel_id=1, source_target_pairs={{0,3},{1,2},{2,1},{3,0},{4,7},{5,6},{6,5},{7,4},{8,11},{9,10},{10,... | collective-permute-start | bytes 6291464 | tf_op jit(solution)/shard_map/ppermute | solution.py:93
  (40 other events, 606.8 us)
